TPU v7x, 32 devices: a whole 2x2x4 slice. The times are simulated.
32 devices in a mesh: freq: 4 (over y, x), bond: 8 (over z, core).
Axes of the slice: x: 2, y: 2, z: 4, core: 2. Of those that a mesh axis runs over, the one named last changes fastest.
Arguments:
- gamma: bfloat16 [2, 8, 32, 384, 384], P(None, 'freq', 'bond'), may hold values from -1 to 1
- green: float32 [2, 8, 32, 256], P(None, 'freq', 'bond'), may hold values from -6 to 6
- single: float32 [2, 8, 32, 256], P(None, 'freq', 'bond'), may hold values from -6 to 6
- bond_site: int32 [384], replicated, may hold values from 0 to 255
- causal_mask: int32 [8, 3, 3], P('freq'), may hold values 0 or 1
- site_perm: int32 [384], replicated, may hold values from 0 to 383, each once
Outputs:
- p_vertex: bfloat16 [2, 8, 384, 32, 384], P(None, 'freq', 'bond')
Inputs may be any that keep to these rules, and one draw needn't show every extreme that they name: `bond_site`: each of the 384 bond-Keldysh indices names one site. `causal_mask`: 1 keeps a causality block of 128 x 128 entries, 0 removes it. `site_perm`: a permutation of the 384 column indices.
All inputs are finite; a program needn't handle non-finite values.
Results may differ from a plain program's by a relative error of at most 0.0049.
Values may be sent and summed in bfloat16 or wider, within the bound.
A program may use at most 128 MiB of HBM per device.

v0:
```python
import math
import jax
import jax.numpy as jnp
from jax import lax
from jax.sharding import PartitionSpec as P


def times_complex(first_real, first_imag, second_real, second_imag):
    return (
        first_real * second_real - first_imag * second_imag,
        first_real * second_imag + first_imag * second_real,
    )


def products(pattern, left, right):
    return jnp.einsum(pattern, left, right, preferred_element_type=jnp.float32)


def complex_flow(pattern, left_real, left_imag, gamma_real, gamma_imag):
    flow_real = products(pattern, left_real, gamma_real) - products(pattern, left_imag, gamma_imag)
    flow_imag = products(pattern, left_real, gamma_imag) + products(pattern, left_imag, gamma_real)
    return (flow_real, flow_imag)


def compute_flows(gamma_part, bubble_part, mask_part, site_perm):
    order = gamma_part.shape[-1]
    blocks = mask_part.shape[-1]
    width = order // blocks
    gamma_real = gamma_part[0].astype(jnp.float32)
    gamma_imag = gamma_part[1].astype(jnp.float32)
    bubble_real = bubble_part[0][:, :, None, :]
    bubble_imag = bubble_part[1][:, :, None, :]
    left_real = (gamma_real * bubble_real - gamma_imag * bubble_imag).astype(jnp.bfloat16)
    left_imag = (gamma_real * bubble_imag + gamma_imag * bubble_real).astype(jnp.bfloat16)
    flow_real, flow_imag = complex_flow(
        "wsrk,wskc->wrsc", left_real, left_imag, gamma_part[0], gamma_part[1]
    )
    spread = jnp.repeat(jnp.repeat(mask_part, width, axis=1), width, axis=2).astype(jnp.float32)
    flow_real = flow_real * spread[:, :, None, :]
    flow_imag = flow_imag * spread[:, :, None, :]
    rounded = jnp.stack([flow_real, flow_imag]).astype(jnp.bfloat16)
    return jnp.take(rounded, site_perm, axis=4)


def body(gamma, green, single, bond_site, causal_mask, site_perm):
    local = green.shape[1]
    count = local * lax.axis_size("freq")
    whole_green, whole_single = (
        lax.all_gather(green, "freq", axis=1, tiled=True),
        lax.all_gather(single, "freq", axis=1, tiled=True),
    )
    green_bond = jnp.take(whole_green, bond_site, axis=3)
    single_bond = jnp.take(whole_single, bond_site, axis=3)
    owned = lax.axis_index("freq") * local + jnp.arange(local, dtype=jnp.int32)
    shifts = (jnp.arange(count, dtype=jnp.int32)[None, :] + owned[:, None]) % count
    green_moved = jnp.take(green_bond, shifts, axis=1)
    single_moved = jnp.take(single_bond, shifts, axis=1)
    first = times_complex(
        green_bond[0][None], green_bond[1][None], single_moved[0], single_moved[1]
    )
    second = times_complex(
        single_bond[0][None], single_bond[1][None], green_moved[0], green_moved[1]
    )
    factor = 1.0 / math.sqrt(count)
    bubble = jnp.stack(
        [
            jnp.sum(first[0] + second[0], axis=1) * factor,
            jnp.sum(first[1] + second[1], axis=1) * factor,
        ]
    )
    flows = compute_flows(gamma, bubble, causal_mask, site_perm)
    return lax.all_to_all(flows, "bond", split_axis=2, concat_axis=3, tiled=True)


def solution(mesh):
    in_specs = (
        P(None, "freq", "bond", None, None),
        P(None, "freq", "bond", None),
        P(None, "freq", "bond", None),
        P(),
        P("freq", None, None),
        P(),
    )
    out_specs = P(None, "freq", "bond", None, None)
    return jax.shard_map(body, mesh=mesh, in_specs=in_specs, out_specs=out_specs, check_vma=False)
```

profile of v0, /device:TPU:0, one launch (start us, length us, event | category | flops | bytes accessed | tf_op | source)
XLA Modules:
  0.0 229.6 jit_solution(18322149337392258693)
XLA Ops:
  0.0 0.7 compare_select_fusion
  0.7 0.7 compare_and_fusion.1
  1.5 0.7 copy.95
  2.3 9.7 %all_gather.6 = f32[2,8,4,256]{3,2,0,1:T(4,128)S(1)} all-gather(f32[2,2,4,256]{3,2,0,1:T(4,128)S(1)} %copy.95), channel_id=1, replica_groups=mesh['freq'=4,'bond'=8] {'freq'}, dimensions={1}, use_global_device_ids=true | all-gather | bytes 81920 | tf_op jit(solution)/shard_map/all_gather | solution.py:49
  12.0 0.4 copy.96
  12.4 0.7 copy.98
  13.1 8.2 %all_gather.7 = f32[2,8,4,256]{3,2,0,1:T(4,128)S(1)} all-gather(f32[2,2,4,256]{3,2,0,1:T(4,128)S(1)} %copy.98), channel_id=1, replica_groups=mesh['freq'=4,'bond'=8] {'freq'}, dimensions={1}, use_global_device_ids=true | all-gather | bytes 81920 | tf_op jit(solution)/shard_map/all_gather | solution.py:50
  21.7 3.1 %gather_fusion.1 = f32[384,2,8,4]{2,3,1,0:T(4,128)} fusion(f32[2,8,4,256]{1,2,3,0:T(4,128)S(1)} %copy.96, s32[1024]{0:T(1024)S(1)} %pad_clamp_fusion.2), kind=kCustom, calls=%fused_computation.clone | custom fusion | bytes 198144 | tf_op jit(solution)/shard_map/jit(_take)/gather | solution.py:52
  24.8 3.1 %gather_fusion.2 = f32[384,2,8,4]{2,3,1,0:T(4,128)} fusion(f32[2,8,4,256]{1,2,3,0:T(4,128)S(1)} %copy.99, s32[1024]{0:T(1024)S(1)} %pad_clamp_fusion.2), kind=kCustom, calls=%fused_computation.2.clone | custom fusion | bytes 198144 | tf_op jit(solution)/shard_map/jit(_take)/gather | solution.py:53
  28.0 2.8 %select_bitcast_fusion.2 = (f32[2,8,4,384]{1,2,0,3:T(4,128)S(1)}, f32[2,8,4,384]{1,2,0,3:T(4,128)S(1)}) fusion(f32[384,2,8,4]{2,3,1,0:T(4,128)} %gather_fusion.1, pred[384]{0:T(512)(128)(4,1)S(1)} %compare_and_fusion.1, f32[384,2,8,4]{2,3,1,0:T(4,128)} %gather_fusion.2), kind=kLoop, calls=%fused_computation.40 | loop fusion | flops 49152 | bytes 393600 | tf_op jit(solution)/shard_map/jit(_take)/select_n | solution.py:52
  30.8 0.8 copy.100
  31.5 1.0 copy.104
  32.5 2.0 slice_bitcast_fusion.1
  34.6 0.7 gather_fusion.3
  35.2 0.7 gather_fusion.4
  35.9 1.4 copy.102
  37.3 1.4 copy.103
  38.7 1.4 copy.106
  40.0 1.4 copy.97
  41.7 7.0 %fusion.6 = f32[2,4,384,384]{3,2,1,0:T(8,128)} fusion(f32[2,4,384]{2,1,0:T(4,128)S(1)} %copy_multiply_fusion, f32[2,4,384]{2,1,0:T(4,128)S(1)} %copy_multiply_fusion.1, bf16[2,2,4,384,384]{4,3,2,1,0:T(8,128)(2,1)} %param.10), kind=kOutput, calls=%fused_computation.18 | convolution fusion | flops 913047552 | bytes 11821056 | tf_op jit(solution)/shard_map/wsrk,wskc->wrsc/dot_general | solution.py:16
  48.7 3.8 %fusion.4 = f32[2,4,384,384]{3,2,1,0:T(8,128)} fusion(f32[2,4,384]{2,1,0:T(4,128)S(1)} %copy_multiply_fusion, f32[2,4,384]{2,1,0:T(4,128)S(1)} %copy_multiply_fusion.1, bf16[2,2,4,384,384]{4,3,2,1,0:T(8,128)(2,1)S(1)} %bitcast.115), kind=kOutput, calls=%fused_computation.17 | convolution fusion | flops 913047552 | bytes 11821056 | tf_op jit(solution)/shard_map/wsrk,wskc->wrsc/dot_general | solution.py:16
  53.2 6.1 %fusion.12 = bf16[1,2,384,4,384]{4,2,3,1,0:T(8,128)(2,1)S(1)} fusion(f32[2,4,384,384]{3,2,1,0:T(8,128)} %fusion.6, f32[2,384,384]{2,1,0:T(8,128)S(1)} %copy.111, f32[2,4,384]{2,1,0:T(4,128)S(1)} %copy_multiply_fusion, f32[2,4,384]{2,1,0:T(4,128)S(1)} %copy_multiply_fusion.1, bf16[2,2,4,384,384]{4,3,2,1,0:T(8,128)(2,1)} %param.10), kind=kOutput, calls=%fused_computation.21 | convolution fusion | flops 916586496 | bytes 15360000 | tf_op jit(solution)/shard_map/wsrk,wskc->wrsc/dot_general | solution.py:16
  59.3 6.1 %fusion.13 = bf16[1,2,384,4,384]{4,2,3,1,0:T(8,128)(2,1)S(1)} fusion(f32[2,4,384,384]{3,2,1,0:T(8,128)} %fusion.4, f32[2,384,384]{2,1,0:T(8,128)S(1)} %copy.111, f32[2,4,384]{2,1,0:T(4,128)S(1)} %copy_multiply_fusion, f32[2,4,384]{2,1,0:T(4,128)S(1)} %copy_multiply_fusion.1, bf16[2,2,4,384,384]{4,3,2,1,0:T(8,128)(2,1)} %param.10), kind=kOutput, calls=%fused_computation.22 | convolution fusion | flops 916586496 | bytes 15360000 | tf_op jit(solution)/shard_map/wsrk,wskc->wrsc/dot_general | solution.py:16
  65.4 2.7 %pad_maximum_fusion = bf16[2,2,384,4,384]{4,2,3,1,0:T(8,128)(2,1)} fusion(bf16[1,2,384,4,384]{4,2,3,1,0:T(8,128)(2,1)S(1)} %fusion.13, bf16[1,2,384,4,384]{4,2,3,1,0:T(8,128)(2,1)S(1)} %fusion.12), kind=kLoop, calls=%fused_computation.13 | loop fusion | flops 2359296 | bytes 9437184 | tf_op jit(solution)/shard_map/stack | solution.py:41
  68.1 8.5 %copy.112 = bf16[2,2,384,4,384]{2,3,4,1,0:T(4,128)(2,1)} copy(bf16[2,2,384,4,384]{4,2,3,1,0:T(8,128)(2,1)} %pad_maximum_fusion) | data formatting | bytes 9437184 | tf_op jit(solution)/shard_map/stack | solution.py:41
  76.6 20.7 %gather_fusion = bf16[384,2,2,384,4]{3,4,2,1,0:T(4,128)(2,1)} fusion(bf16[2,2,384,4,384]{2,3,4,1,0:T(4,128)(2,1)} %copy.112, s32[1024]{0:T(1024)S(1)} %pad_clamp_fusion), kind=kCustom, calls=%fused_computation.4 | custom fusion | bytes 9438720 | tf_op jit(solution)/shard_map/jit(_take)/gather | solution.py:42
  97.3 6.8 %select_bitcast_fusion = bf16[2,2,384,4,384]{2,3,1,0,4:T(4,128)(2,1)} fusion(bf16[384,2,2,384,4]{3,4,2,1,0:T(4,128)(2,1)} %gather_fusion, pred[384]{0:T(512)(128)(4,1)S(1)} %compare_and_fusion.2), kind=kLoop, calls=%fused_computation.14 | loop fusion | flops 2359296 | bytes 9437568 | tf_op jit(solution)/shard_map/jit(_take)/select_n | solution.py:42
  104.1 10.3 %copy.113 = bf16[2,2,384,4,384]{4,3,1,0,2:T(4,128)(2,1)} copy(bf16[2,2,384,4,384]{2,3,1,0,4:T(4,128)(2,1)} %select_bitcast_fusion) | data formatting | bytes 9437184 | tf_op jit(solution)/shard_map/jit(_take)/select_n | solution.py:42
  114.4 110.1 %all_to_all.18 = bf16[2,2,384,4,384]{4,3,1,0,2:T(4,128)(2,1)S(1)} all-to-all(bf16[2,2,384,4,384]{4,3,1,0,2:T(4,128)(2,1)} %copy.113), channel_id=1, replica_groups=mesh['freq'=4,'bond'=8] {'bond'}, dimensions={2} | all-to-all | bytes 9437184 | tf_op jit(solution)/shard_map/all_to_all | solution.py:72
  224.5 1.1 copy.114
  225.6 0.8 copy.115
  226.4 3.2 %copy.116 = bf16[2,2,48,32,384]{4,3,2,1,0:T(8,128)(2,1)} copy(bf16[2,2,48,32,384]{4,2,3,1,0:T(8,128)(2,1)S(1)} %bitcast.112) | data formatting | bytes 9437184 | tf_op jit(solution)/shard_map/all_to_all | solution.py:72
  (30 shorter events, 1.6 us)
Async XLA Ops:
  41.5 7.1 %slice-start = ((s8[4718592]{0:T(1024)(128)(4,1)}), s8[4194304]{0:T(1024)(128)(4,1)S(1)}, s32[]{:S(2)}) async-start(s8[4718592]{0:T(1024)(128)(4,1)} %bitcast.114), calls=%async_computation.1 | async-start | bytes 8388608
  41.7 7.0 %slice-start.1 = ((s8[4718592]{0:T(1024)(128)(4,1)}), s8[524288]{0:T(1024)(128)(4,1)S(1)}, s32[]{:S(2)}) async-start(s8[4718592]{0:T(1024)(128)(4,1)} %bitcast.114), calls=%async_computation.2 | async-start | bytes 1048576
  48.7 3.8 %copy-start = (s32[384]{0:T(512)S(1)}, s32[384]{0:T(512)}, u32[]{:S(2)}) copy-start(s32[384]{0:T(512)} %param.15) | copy-start | bytes 4612
  48.7 3.8 %copy-start.1 = (s32[2,3,3]{2,0,1:T(2,128)S(1)}, s32[2,3,3]{2,0,1:T(2,128)}, u32[]{:S(2)}) copy-start(s32[2,3,3]{2,0,1:T(2,128)} %param.14) | copy-start | bytes 220
where the time goes:
time: 231 us; the launch traced here: 230 us
  blocking collectives  128 us (55%)
  local copies, waits for them, and re-layouts  64.3 us (28%)
  matrix products  23 us (10%)
  other arithmetic  14.1 us (6%)
    all_to_all x1, blocking collectives, body(): lax.all_to_all(flows, 'bond', split_axis=2, concat_axis=3, tiled=True)  110 us
    dot_general x4, matrix products, products(): return jnp.einsum(pattern, left, right, preferred_element_type=jnp.float32)  23 us
    gather x1, local copies, waits for them, and re-layouts, compute_flows(): return jnp.take(rounded, site_perm, axis=4)  20.7 us
    select_n x1, local copies, waits for them, and re-layouts, compute_flows(): return jnp.take(rounded, site_perm, axis=4)  10.3 us
    all_gather x1, blocking collectives, body(): lax.all_gather(green, 'freq', axis=1, tiled=True)  9.71 us
    another operation x1, local copies, waits for them, and re-layouts, compute_flows(): rounded = jnp.stack([flow_real, flow_imag]).astype(jnp.bfloat16)  8.47 us
    all_gather x1, blocking collectives, body(): lax.all_gather(single, 'freq', axis=1, tiled=True)  8.2 us
    select_n x2, other arithmetic, compute_flows(): return jnp.take(rounded, site_perm, axis=4)  6.84 us

commit v1 on v0

--- a/solution.py
+++ b/solution.py
@@ -69,7 +69,10 @@
         ]
     )
     flows = compute_flows(gamma, bubble, causal_mask, site_perm)
-    return lax.all_to_all(flows, "bond", split_axis=2, concat_axis=3, tiled=True)
+    return jnp.concatenate(
+        lax.all_to_all(jnp.stack(jnp.split(flows, lax.axis_size("bond"), axis=2)), "bond", 0, 0),
+        axis=3,
+    )
 
 
 def solution(mesh):

time: 231 us -> 258 us (1.12)
  local copies, waits for them, and re-layouts: 64.3 us -> 92.3 us
    another operation x0 -> x10, local copies, waits for them, and re-layouts: none -> 34.6 us  [body(): jnp.stack(jnp.split(flows, lax.axis_size('bond'), axis=2))]
    select_n x1 -> x0, local copies, waits for them, and re-layouts: 10.3 us -> none  [compute_flows(): return jnp.take(rounded, site_perm, axis=4)]
    unnamed x10 -> x23, local copies, waits for them, and re-layouts: 1.47 us -> 6.45 us
    all_to_all x3 -> x1, local copies, waits for them, and re-layouts: 5.12 us -> 0.6 us  [body(): lax.all_to_all(jnp.stack(jnp.split(flows, lax.axis_size('bond'), axis=2))...]
    reshape x0 -> x1, local copies, waits for them, and re-layouts: none -> 3.21 us  [body(): jnp.concatenate(lax.all_to_all(jnp.stack(jnp.split(flows, lax.axis_size('...]
where the time goes in v1:
time: 258 us; the launch traced here: 257 us
  blocking collectives  128 us (50%)
  local copies, waits for them, and re-layouts  92.3 us (36%)
  matrix products  23 us (9%)
  other arithmetic  13.3 us (5%)
    all_to_all x1, blocking collectives, body(): lax.all_to_all(jnp.stack(jnp.split(flows, lax.axis_size('bond'), axis=2))...  110 us
    another operation x10, local copies, waits for them, and re-layouts, body(): jnp.stack(jnp.split(flows, lax.axis_size('bond'), axis=2))  34.6 us
    dot_general x4, matrix products, products(): return jnp.einsum(pattern, left, right, preferred_element_type=jnp.float32)  23 us
    gather x1, local copies, waits for them, and re-layouts, compute_flows(): return jnp.take(rounded, site_perm, axis=4)  20.7 us
    all_gather x1, blocking collectives, body(): lax.all_gather(single, 'freq', axis=1, tiled=True)  9.71 us
    another operation x1, local copies, waits for them, and re-layouts, compute_flows(): rounded = jnp.stack([flow_real, flow_imag]).astype(jnp.bfloat16)  8.46 us
    all_gather x1, blocking collectives, body(): lax.all_gather(green, 'freq', axis=1, tiled=True)  8.21 us
    unnamed x23, local copies, waits for them, and re-layouts  6.45 us

profile of v1, /device:TPU:0, one launch (start us, length us, event | category | flops | bytes accessed | tf_op | source)
XLA Modules:
  0.0 256.7 jit_solution(12801464151597070704)
XLA Ops:
  4.4 9.7 %all_gather.7 = f32[2,8,4,256]{3,2,0,1:T(4,128)S(1)} all-gather(f32[2,2,4,256]{3,2,0,1:T(4,128)S(1)} %copy.66), channel_id=1, replica_groups=mesh['freq'=4,'bond'=8] {'freq'}, dimensions={1}, use_global_device_ids=true | all-gather | bytes 81920 | tf_op jit(solution)/shard_map/all_gather | solution.py:50
  14.1 8.2 %all_gather.6 = f32[2,8,4,256]{3,2,0,1:T(4,128)S(1)} all-gather(f32[2,2,4,256]{3,2,0,1:T(4,128)S(1)} %copy.63), channel_id=1, replica_groups=mesh['freq'=4,'bond'=8] {'freq'}, dimensions={1}, use_global_device_ids=true | all-gather | bytes 81920 | tf_op jit(solution)/shard_map/all_gather | solution.py:49
  23.1 3.1 %gather_fusion.1 = f32[384,2,8,4]{2,3,1,0:T(4,128)} fusion(f32[2,8,4,256]{1,2,3,0:T(4,128)S(1)} %copy.64, s32[1024]{0:T(1024)S(1)} %pad_clamp_fusion.2), kind=kCustom, calls=%fused_computation.clone | custom fusion | bytes 198144 | tf_op jit(solution)/shard_map/jit(_take)/gather | solution.py:52
  26.2 3.2 %gather_fusion.2 = f32[384,2,8,4]{2,3,1,0:T(4,128)} fusion(f32[2,8,4,256]{1,2,3,0:T(4,128)S(1)} %copy.67, s32[1024]{0:T(1024)S(1)} %pad_clamp_fusion.2), kind=kCustom, calls=%fused_computation.2.clone | custom fusion | bytes 198144 | tf_op jit(solution)/shard_map/jit(_take)/gather | solution.py:53
  29.4 2.8 %select_bitcast_fusion.2 = (f32[2,8,4,384]{1,2,0,3:T(4,128)S(1)}, f32[2,8,4,384]{1,2,0,3:T(4,128)S(1)}) fusion(f32[384,2,8,4]{2,3,1,0:T(4,128)} %gather_fusion.1, pred[384]{0:T(512)(128)(4,1)S(1)} %compare_and_fusion.1, f32[384,2,8,4]{2,3,1,0:T(4,128)} %gather_fusion.2), kind=kLoop, calls=%fused_computation.48 | loop fusion | flops 49152 | bytes 393600 | tf_op jit(solution)/shard_map/jit(_take)/select_n | solution.py:52
  33.9 1.9 slice_bitcast_fusion.9
  35.9 1.4 copy.71
  37.3 1.4 copy.74
  38.6 1.4 copy.70
  40.0 1.4 copy.65
  43.1 7.0 %fusion.6 = f32[2,4,384,384]{3,2,1,0:T(8,128)} fusion(f32[2,4,384]{2,1,0:T(4,128)S(1)} %copy_multiply_fusion, f32[2,4,384]{2,1,0:T(4,128)S(1)} %copy_multiply_fusion.1, bf16[2,2,4,384,384]{4,3,2,1,0:T(8,128)(2,1)} %param.10), kind=kOutput, calls=%fused_computation.18 | convolution fusion | flops 913047552 | bytes 11821056 | tf_op jit(solution)/shard_map/wsrk,wskc->wrsc/dot_general | solution.py:16
  50.0 3.8 %fusion.4 = f32[2,4,384,384]{3,2,1,0:T(8,128)} fusion(f32[2,4,384]{2,1,0:T(4,128)S(1)} %copy_multiply_fusion, f32[2,4,384]{2,1,0:T(4,128)S(1)} %copy_multiply_fusion.1, bf16[2,2,4,384,384]{4,3,2,1,0:T(8,128)(2,1)S(1)} %bitcast.129), kind=kOutput, calls=%fused_computation.17 | convolution fusion | flops 913047552 | bytes 11821056 | tf_op jit(solution)/shard_map/wsrk,wskc->wrsc/dot_general | solution.py:16
  54.5 6.1 %fusion.12 = bf16[1,2,384,4,384]{4,2,3,1,0:T(8,128)(2,1)S(1)} fusion(f32[2,4,384,384]{3,2,1,0:T(8,128)} %fusion.6, f32[2,384,384]{2,1,0:T(8,128)S(1)} %copy.79, f32[2,4,384]{2,1,0:T(4,128)S(1)} %copy_multiply_fusion, f32[2,4,384]{2,1,0:T(4,128)S(1)} %copy_multiply_fusion.1, bf16[2,2,4,384,384]{4,3,2,1,0:T(8,128)(2,1)} %param.10), kind=kOutput, calls=%fused_computation.21 | convolution fusion | flops 916586496 | bytes 15360000 | tf_op jit(solution)/shard_map/wsrk,wskc->wrsc/dot_general | solution.py:16
  60.6 6.1 %fusion.13 = bf16[1,2,384,4,384]{4,2,3,1,0:T(8,128)(2,1)S(1)} fusion(f32[2,4,384,384]{3,2,1,0:T(8,128)} %fusion.4, f32[2,384,384]{2,1,0:T(8,128)S(1)} %copy.79, f32[2,4,384]{2,1,0:T(4,128)S(1)} %copy_multiply_fusion, f32[2,4,384]{2,1,0:T(4,128)S(1)} %copy_multiply_fusion.1, bf16[2,2,4,384,384]{4,3,2,1,0:T(8,128)(2,1)} %param.10), kind=kOutput, calls=%fused_computation.22 | convolution fusion | flops 916586496 | bytes 15360000 | tf_op jit(solution)/shard_map/wsrk,wskc->wrsc/dot_general | solution.py:16
  66.7 2.7 %pad_maximum_fusion = bf16[2,2,384,4,384]{4,2,3,1,0:T(8,128)(2,1)} fusion(bf16[1,2,384,4,384]{4,2,3,1,0:T(8,128)(2,1)S(1)} %fusion.13, bf16[1,2,384,4,384]{4,2,3,1,0:T(8,128)(2,1)S(1)} %fusion.12), kind=kLoop, calls=%fused_computation.13 | loop fusion | flops 2359296 | bytes 9437184 | tf_op jit(solution)/shard_map/stack | solution.py:41
  69.4 8.5 %copy.80 = bf16[2,2,384,4,384]{2,3,4,1,0:T(4,128)(2,1)} copy(bf16[2,2,384,4,384]{4,2,3,1,0:T(8,128)(2,1)} %pad_maximum_fusion) | data formatting | bytes 9437184 | tf_op jit(solution)/shard_map/stack | solution.py:41
  77.9 20.7 %gather_fusion = bf16[384,2,2,384,4]{3,4,2,1,0:T(4,128)(2,1)} fusion(bf16[2,2,384,4,384]{2,3,4,1,0:T(4,128)(2,1)} %copy.80, s32[1024]{0:T(1024)S(1)} %get-tuple-element.25), kind=kCustom, calls=%fused_computation.4 | custom fusion | bytes 9438720 | tf_op jit(solution)/shard_map/jit(_take)/gather | solution.py:42
  98.6 4.7 %select_bitcast_fusion = bf16[2,2,384,4,384]{2,3,1,0,4:T(4,128)(2,1)S(1)} fusion(bf16[384,2,2,384,4]{3,4,2,1,0:T(4,128)(2,1)} %gather_fusion, pred[384]{0:T(512)(128)(4,1)S(1)} %compare_and_fusion.2), kind=kLoop, calls=%fused_computation.14 | loop fusion | flops 2359296 | bytes 9437568 | tf_op jit(solution)/shard_map/jit(_take)/select_n | solution.py:42
  103.3 8.0 %slice_bitcast_fusion = (bf16[1,2,2,48,4,384]{3,4,2,1,5,0:T(4,128)(2,1)}, bf16[1,2,2,48,4,384]{3,4,2,1,5,0:T(4,128)(2,1)}, bf16[1,2,2,48,4,384]{3,4,2,1,5,0:T(4,...) fusion(bf16[2,2,384,4,384]{2,3,1,0,4:T(4,128)(2,1)S(1)} %select, ...), kind=kLoop, calls=%fused_computation.39 | loop fusion | bytes 9437184 | tf_op jit(solution)/shard_map/stack | solution.py:73
  111.3 3.7 %copy.88 = bf16[1,2,2,48,4,384]{5,3,4,2,1,0:T(8,128)(2,1)} copy(bf16[1,2,2,48,4,384]{3,4,2,1,5,0:T(4,128)(2,1)} %get-tuple-element.9) | data formatting | bytes 1179648 | tf_op jit(solution)/shard_map/stack | solution.py:73
  115.0 3.7 %copy.87 = bf16[1,2,2,48,4,384]{5,3,4,2,1,0:T(8,128)(2,1)} copy(bf16[1,2,2,48,4,384]{3,4,2,1,5,0:T(4,128)(2,1)} %get-tuple-element.10) | data formatting | bytes 1179648 | tf_op jit(solution)/shard_map/stack | solution.py:73
  118.6 3.7 %copy.86 = bf16[1,2,2,48,4,384]{5,3,4,2,1,0:T(8,128)(2,1)} copy(bf16[1,2,2,48,4,384]{3,4,2,1,5,0:T(4,128)(2,1)} %get-tuple-element.11) | data formatting | bytes 1179648 | tf_op jit(solution)/shard_map/stack | solution.py:73
  122.3 3.7 %copy.85 = bf16[1,2,2,48,4,384]{5,3,4,2,1,0:T(8,128)(2,1)} copy(bf16[1,2,2,48,4,384]{3,4,2,1,5,0:T(4,128)(2,1)} %get-tuple-element.12) | data formatting | bytes 1179648 | tf_op jit(solution)/shard_map/stack | solution.py:73
  126.0 3.7 %copy.84 = bf16[1,2,2,48,4,384]{5,3,4,2,1,0:T(8,128)(2,1)} copy(bf16[1,2,2,48,4,384]{3,4,2,1,5,0:T(4,128)(2,1)} %get-tuple-element.13) | data formatting | bytes 1179648 | tf_op jit(solution)/shard_map/stack | solution.py:73
  129.6 3.7 %copy.83 = bf16[1,2,2,48,4,384]{5,3,4,2,1,0:T(8,128)(2,1)} copy(bf16[1,2,2,48,4,384]{3,4,2,1,5,0:T(4,128)(2,1)} %get-tuple-element.14) | data formatting | bytes 1179648 | tf_op jit(solution)/shard_map/stack | solution.py:73
  133.3 2.3 copy.82
  135.6 2.2 copy.81
  137.8 1.2 constant_dynamic-update-slice_fusion.7
  139.0 1.2 constant_dynamic-update-slice_fusion.6
  140.2 1.2 constant_dynamic-update-slice_fusion.5
  143.0 109.9 %all_to_all.5 = bf16[8,2,2,48,4,384]{5,3,4,2,1,0:T(8,128)(2,1)S(1)} all-to-all(bf16[8,2,2,48,4,384]{5,3,4,2,1,0:T(8,128)(2,1)S(1)} %constant_dynamic-update-slice_fusion), channel_id=1, replica_groups=mesh['freq'=4,'bond'=8] {'bond'}, dimensions={0} | all-to-all | bytes 9437184 | tf_op jit(solution)/shard_map/all_to_all | solution.py:73
  253.5 3.2 %copy.90 = bf16[2,2,48,32,384]{4,3,2,1,0:T(8,128)(2,1)} copy(bf16[2,2,48,32,384]{4,2,3,1,0:T(8,128)(2,1)S(1)} %bitcast.126) | data formatting | bytes 9437184 | tf_op jit(solution)/shard_map/reshape | solution.py:72
  (50 shorter events, 11.4 us)
Async XLA Ops:
  42.9 7.2 %slice-start = ((s8[4718592]{0:T(1024)(128)(4,1)}), s8[4194304]{0:T(1024)(128)(4,1)S(1)}, s32[]{:S(2)}) async-start(s8[4718592]{0:T(1024)(128)(4,1)} %bitcast.128), calls=%async_computation.1 | async-start | bytes 8388608
  43.0 7.0 %slice-start.1 = ((s8[4718592]{0:T(1024)(128)(4,1)}), s8[524288]{0:T(1024)(128)(4,1)S(1)}, s32[]{:S(2)}) async-start(s8[4718592]{0:T(1024)(128)(4,1)} %bitcast.128), calls=%async_computation.2 | async-start | bytes 1048576
  50.0 3.8 %copy-start.4 = (s32[2,3,3]{2,0,1:T(2,128)S(1)}, s32[2,3,3]{2,0,1:T(2,128)}, u32[]{:S(2)}) copy-start(s32[2,3,3]{2,0,1:T(2,128)} %param.14) | copy-start | bytes 220
  135.6 7.1 %copy-start.2 = (bf16[1,2,2,48,4,384]{5,3,4,2,1,0:T(8,128)(2,1)S(1)}, bf16[1,2,2,48,4,384]{5,3,4,2,1,0:T(8,128)(2,1)}, u32[]{:S(2)}) copy-start(bf16[1,2,2,48,4,384]{5,3,4,2,1,0:T(8,128)(2,1)} %copy.86) | copy-start | bytes 1769476
  135.6 7.2 %copy-start.1 = (bf16[1,2,2,48,4,384]{5,3,4,2,1,0:T(8,128)(2,1)S(1)}, bf16[1,2,2,48,4,384]{5,3,4,2,1,0:T(8,128)(2,1)}, u32[]{:S(2)}) copy-start(bf16[1,2,2,48,4,384]{5,3,4,2,1,0:T(8,128)(2,1)} %copy.87) | copy-start | bytes 1769476
  135.6 7.3 %copy-start = (bf16[1,2,2,48,4,384]{5,3,4,2,1,0:T(8,128)(2,1)S(1)}, bf16[1,2,2,48,4,384]{5,3,4,2,1,0:T(8,128)(2,1)}, u32[]{:S(2)}) copy-start(bf16[1,2,2,48,4,384]{5,3,4,2,1,0:T(8,128)(2,1)} %copy.88) | copy-start | bytes 1769476
  137.8 4.7 %copy-start.3 = (bf16[1,2,2,48,4,384]{5,3,4,2,1,0:T(8,128)(2,1)S(1)}, bf16[1,2,2,48,4,384]{5,3,4,2,1,0:T(8,128)(2,1)}, u32[]{:S(2)}) copy-start(bf16[1,2,2,48,4,384]{5,3,4,2,1,0:T(8,128)(2,1)} %copy.85) | copy-start | bytes 1769476
